TPU v7x, 32 devices: a whole 2x2x4 slice. The times are simulated.
32 devices in a mesh: sta: 4 (over y, x), evt: 8 (over z, core).
Axes of the slice: x: 2, y: 2, z: 4, core: 2. Of those that a mesh axis runs over, the one named last changes fastest.
Arguments:
- traces: bfloat16 [3, 32, 512, 2048], P(None, 'sta', 'evt'), may hold values from -96 to 96
- baz_bin: int32 [32, 512], P('sta', 'evt'), may hold values from 0 to 35
- inc_bin: int32 [32, 512], P('sta', 'evt'), may hold values from 0 to 7
- counts: int32 [32], P('sta'), may hold values from 64 to 512
- depth_index: int32 [32, 512], P('sta'), may hold values from 0 to 2046
- tile_of: int32 [32], replicated, may hold values from 0 to 15
Outputs:
- stack: float32 [16, 5, 2, 512], P('sta', None, None, 'evt')
All inputs are finite; a program needn't handle non-finite values.
Results may differ from a plain program's by a relative error of at most 0.0003.
Values sent between devices are 32-bit elements; how exact they have to be, the bound alone decides.
A program may use at most 64 MiB of HBM per device.

v0:
```python
import jax
import jax.numpy as jnp
from jax import lax
from jax.sharding import PartitionSpec as P

NS = 2048
DEPTHS = 512
BAZ_BINS = 36
TILE_DEV = 4


def solve_blocks(normal, right):
    factor = jnp.linalg.cholesky(normal)
    middle = jax.scipy.linalg.solve_triangular(factor, right, lower=True)
    return jax.scipy.linalg.solve_triangular(factor, middle, lower=True, trans=1)


def to_depths(values, indices):
    picks = indices[:, None, None, :]
    first = jnp.take_along_axis(values, picks, axis=3)
    second = jnp.take_along_axis(values, picks + 1, axis=3)
    return 0.5 * (first + second)


def body(traces, baz_bin, inc_bin, counts, depth_index, tile_of):
    highest = lax.Precision.HIGHEST
    stations = traces.shape[1]
    slots = traces.shape[2]
    evt_count = lax.axis_size("evt")
    depth_share = DEPTHS // evt_count
    phi = (baz_bin.astype(jnp.float32) + 0.5) * (2.0 * jnp.pi / BAZ_BINS)
    incidence = (12.0 + 2.5 * (inc_bin.astype(jnp.float32) + 0.5)) * (jnp.pi / 180.0)
    cosine = jnp.cos(phi)[:, :, None]
    sine = jnp.sin(phi)[:, :, None]
    vertical = traces[0].astype(jnp.float32)
    north = traces[1].astype(jnp.float32)
    east = traces[2].astype(jnp.float32)
    radial = -(cosine * north + sine * east)
    quality = jnp.cos(incidence)[:, :, None] * radial + jnp.sin(incidence)[:, :, None] * vertical
    transverse = sine * north - cosine * east
    data = jnp.concatenate([quality, transverse], axis=2)
    slot_ids = lax.axis_index("evt") * slots + jnp.arange(slots)
    live = (slot_ids[None, :] < counts[:, None]).astype(jnp.float32)
    harm = jnp.stack(
        [jnp.ones_like(phi), jnp.cos(phi), jnp.sin(phi), jnp.cos(2.0 * phi), jnp.sin(2.0 * phi)],
        axis=2,
    )
    weighted = harm * live[:, :, None]
    normal_part = jnp.einsum("sek,sel->skl", weighted, harm, precision=highest)
    rhs_part = jnp.einsum("sek,sec->skc", weighted, data, precision=highest)
    normal = lax.psum(normal_part, "evt") + jnp.eye(5, dtype=jnp.float32)[None]
    shares = lax.psum_scatter(rhs_part, "evt", scatter_dimension=2, tiled=True)
    solved = solve_blocks(normal, shares)
    coeff = lax.all_gather(solved, "evt", axis=2, tiled=True).reshape(stations, 5, 2, NS)
    mine = lax.dynamic_slice_in_dim(
        depth_index, lax.axis_index("evt") * depth_share, depth_share, 1
    )
    profile = to_depths(coeff, mine)
    first_tile = lax.axis_index("sta") * TILE_DEV
    own_tiles = first_tile + jnp.arange(TILE_DEV)
    members = jnp.sum((tile_of[None, :] == own_tiles[:, None]).astype(jnp.float32), axis=1)
    everyone = lax.all_gather(profile, "sta", axis=0, tiled=True)
    onehot = (tile_of[None, :] == own_tiles[:, None]).astype(jnp.float32)
    sums = jnp.einsum("ts,skcz->tkcz", onehot, everyone, precision=highest)
    return sums / jnp.maximum(members, 1.0)[:, None, None, None]


def solution(mesh):
    return jax.shard_map(
        body,
        mesh=mesh,
        in_specs=(
            P(None, "sta", "evt", None),
            P("sta", "evt"),
            P("sta", "evt"),
            P("sta"),
            P("sta", None),
            P(),
        ),
        out_specs=P("sta", None, None, "evt"),
        check_vma=False,
    )
```

profile of v0, /device:TPU:0, one launch (start us, length us, event | category | flops | bytes accessed | tf_op | source)
XLA Modules:
  0.0 130.2 jit_solution(14801742810654873437)
XLA Ops:
  6.5 0.0 reduce-scatter.2.cloned.1.call-start
  6.5 0.8 fusion.24
  7.3 0.7 compare_convert_fusion
  8.0 6.8 %fusion.7 = (f32[8,64,2048]{2,1,0:T(8,128)}, f32[8,64,2048]{2,1,0:T(8,128)}) fusion(bf16[3,8,64,2048]{3,2,1,0:T(8,128)(2,1)} %param.8, f32[8,64]{1,0:T(8,128)S(1)} %get-tuple-element.18, f32[8,64]{1,0:T(8,128)S(1)} %get-tuple-element.13, f32[8,64]{1,0:T(8,128)S(1)} %get-tuple-element.15, f32[8,64]{1,0:T(8,128)S(1)} %get-tuple-element.19), kind=kLoop, calls=%fused_computation.13 | loop fusion | flops 13631488 | bytes 14688256 | tf_op jit(solution)/shard_map/add | solution.py:39
  14.9 0.0 copy-start
  14.9 0.0 copy-start.1
  14.9 7.3 %fusion = f32[8,5,4096]{2,1,0:T(8,128)} fusion(f32[8,64,2048]{2,1,0:T(8,128)} %get-tuple-element.7, f32[8,64,2048]{2,1,0:T(8,128)} %get-tuple-element.6, f32[8,64,5]{1,2,0:T(8,128)S(1)} %stack.19, f32[8,64]{1,0:T(8,128)S(1)} %compare_convert_fusion), kind=kOutput, calls=%fused_computation.2 | convolution fusion | flops 127928832 | bytes 9056256 | tf_op jit(solution)/shard_map/sek,sec->skc/dot_general | solution.py:50
  22.2 0.0 reduce-scatter.2.cloned.1.call-update
  22.2 0.2 fusion.10
  22.4 30.3 %psum.7 = f32[8,5,5]{1,2,0:T(8,128)S(1)} all-reduce(f32[8,5,5]{1,2,0:T(8,128)S(1)} %fusion.10), channel_id=1, replica_groups=mesh['sta'=4,'evt'=8] {'evt'}, use_global_device_ids=true, to_apply=%region_0.0 | all-reduce | flops 200 | bytes 1600 | tf_op jit(solution)/shard_map/psum | solution.py:51
  52.8 0.1 copy.30
  52.9 0.1 copy.31
  53.0 3.7 %custom-call.11 = f32[8,5,5]{2,1,0:T(8,128)S(1)} custom-call(f32[8,5,5]{2,1,0:T(8,128)S(1)} %fusion.17), custom_call_target="Cholesky" | custom-call | tf_op jit(solution)/shard_map/jit(cholesky)/cholesky | solution.py:13
  56.7 0.1 compare_reduce_fusion
  56.9 0.1 select_bitcast_fusion
  56.9 3.2 %custom-call.12 = f32[8,1,5,5]{2,3,1,0:T(8,128)S(1)} custom-call(f32[8,1,5,5]{3,2,1,0:T(8,128)S(1)} %select_bitcast_fusion), custom_call_target="InvertDiagBlocksLowerTriangular" | custom-call | tf_op jit(solution)/shard_map/jit(_solve_triangular)/vmap()/triangular_solve | solution.py:15
  60.1 0.0 copy-done
  60.1 0.1 bitcast_or_fusion.1
  60.2 0.1 reshape.123
  60.3 0.1 reshape.128
  60.4 0.1 and_bitcast_fusion.1
  60.5 0.0 copy-done.1
  60.5 0.2 fusion.28
  60.7 0.0 reduce-scatter.2.cloned.1.call-done
  60.7 1.2 fusion.15
  61.9 0.3 fusion.13
  62.2 16.4 %all_gather.6 = f32[8,5,4096]{2,1,0:T(8,128)S(1)} all-gather(f32[8,5,512]{2,1,0:T(8,128)S(1)} %fusion.13), channel_id=1, replica_groups=mesh['sta'=4,'evt'=8] {'evt'}, dimensions={2}, use_global_device_ids=true | all-gather | bytes 737280 | tf_op jit(solution)/shard_map/all_gather | solution.py:54
  78.5 0.6 reshape.133
  79.1 17.0 %copy.34 = f32[8,5,2,2048]{1,2,3,0:T(2,128)} copy(f32[8,5,2,2048]{3,2,1,0:T(2,128)S(1)} %reshape.133) | data formatting | bytes 1310720 | tf_op jit(solution)/shard_map/reshape | solution.py:54
  96.1 8.3 %gather_fusion = f32[512,5,2]{1,2,0:T(2,128)S(1)} fusion(f32[8,5,2,2048]{1,2,3,0:T(2,128)} %copy.34, s32[512]{0:T(512)S(1)} %reshape.123), kind=kCustom, calls=%fused_computation.clone | custom fusion | bytes 45056 | tf_op jit(solution)/shard_map/jit(take_along_axis)/gather | solution.py:20
  104.4 0.2 copy.44
  104.6 8.3 %gather_fusion.1 = f32[512,5,2]{1,2,0:T(2,128)S(1)} fusion(f32[8,5,2,2048]{1,2,3,0:T(2,128)} %copy.34, s32[512]{0:T(512)S(1)} %reshape.128), kind=kCustom, calls=%fused_computation.1.clone | custom fusion | bytes 45056 | tf_op jit(solution)/shard_map/jit(take_along_axis)/gather | solution.py:21
  113.0 0.2 copy.46
  113.2 9.3 %all_gather.7 = f32[32,5,2,64]{3,0,2,1:T(8,128)S(1)} all-gather(f32[8,5,2,64]{3,0,2,1:T(8,128)S(1)} %fusion.12), channel_id=1, replica_groups=mesh['sta'=4,'evt'=8] {'sta'}, dimensions={0}, use_global_device_ids=true | all-gather | bytes 102400 | tf_op jit(solution)/shard_map/all_gather | solution.py:62
  122.6 0.2 convolution_divide_fusion
  122.8 0.6 copy.38
  (12 shorter events, 0.1 us)
Async XLA Ops:
  6.5 54.2 %reduce-scatter.2.cloned.1.call-start = ((), (), s32[]{:S(2)}) async-start(), calls=%async_computation.1 | async-start | bytes 1179648 | tf_op jit(solution)/shard_map/reduce_scatter | solution.py:52
  14.9 45.2 %copy-start = (s32[8,512]{1,0:T(8,128)S(1)}, s32[8,512]{1,0:T(8,128)}, u32[]{:S(2)}) copy-start(s32[8,512]{1,0:T(8,128)} %param.12) | copy-start | bytes 49156
  14.9 45.6 %copy-start.1 = (s32[32]{0:T(128)S(1)}, s32[32]{0:T(128)}, u32[]{:S(2)}) copy-start(s32[32]{0:T(128)} %param.13) | copy-start | bytes 388
Sparse Core Ops, SparseCore 0:
  22.3 35.4 reduce-scatter.1
where the time goes:
time: 131 us; the launch traced here: 130 us
  blocking collectives  56 us (43%)
  local copies, waits for them, and re-layouts  35.7 us (27%)
  other arithmetic  15.8 us (12%)
  between operations  13.5 us (10%)
  matrix products  9.13 us (7%)
    psum x1, blocking collectives, body(): normal = lax.psum(normal_part, 'evt') + jnp.eye(5, dtype=jnp.float32)[None]  30.3 us
    reshape x2, local copies, waits for them, and re-layouts, body(): lax.all_gather(solved, 'evt', axis=2, tiled=True)  17.5 us
    all_gather x1, blocking collectives, body(): lax.all_gather(solved, 'evt', axis=2, tiled=True)  16.4 us
    all_gather x1, blocking collectives, body(): everyone = lax.all_gather(profile, 'sta', axis=0, tiled=True)  9.34 us
    gather x3, local copies, waits for them, and re-layouts, to_depths(): second = jnp.take_along_axis(values, picks + 1, axis=3)  8.62 us
    gather x3, local copies, waits for them, and re-layouts, to_depths(): first = jnp.take_along_axis(values, picks, axis=3)  8.62 us
    dot_general x1, matrix products, body(): rhs_part = jnp.einsum('sek,sec->skc', weighted, data, precision=highest)  7.27 us
    add x1, other arithmetic, body(): jnp.cos(incidence)[:, :, None] * radial  6.81 us
  transfers between devices with their start and end apart: 1, of which 0 were waited for; matrix products, arithmetic and copies ran while one was open for 6% of the time, Pallas kernels for 0%

commit v1 on v0

--- a/solution.py
+++ b/solution.py
@@ -59,9 +59,36 @@
     first_tile = lax.axis_index("sta") * TILE_DEV
     own_tiles = first_tile + jnp.arange(TILE_DEV)
     members = jnp.sum((tile_of[None, :] == own_tiles[:, None]).astype(jnp.float32), axis=1)
-    everyone = lax.all_gather(profile, "sta", axis=0, tiled=True)
     onehot = (tile_of[None, :] == own_tiles[:, None]).astype(jnp.float32)
-    sums = jnp.einsum("ts,skcz->tkcz", onehot, everyone, precision=highest)
+    out_arr, carry, low = (lax.psum(1, "sta"), lax.axis_index("sta"), profile.shape[0])
+    log = [(w, (w + 1) % out_arr) for w in range(out_arr)]
+    found = [(w, (w - 1) % out_arr) for w in range(out_arr)]
+    big = out_arr // 2
+    u_next = block_out = profile
+    sums = jnp.einsum(
+        "ts,skcz->tkcz",
+        lax.dynamic_slice_in_dim(onehot, carry * low, profile.shape[0], axis=1),
+        profile,
+        precision=highest,
+    )
+    for c in range(1, big + 1):
+        u_next = lax.ppermute(u_next, "sta", log)
+        if c < out_arr - big:
+            block_out = lax.ppermute(block_out, "sta", found)
+            sums = sums + jnp.einsum(
+                "ts,skcz->tkcz",
+                lax.dynamic_slice_in_dim(
+                    onehot, (carry + c) % out_arr * low, block_out.shape[0], axis=1
+                ),
+                block_out,
+                precision=highest,
+            )
+        sums = sums + jnp.einsum(
+            "ts,skcz->tkcz",
+            lax.dynamic_slice_in_dim(onehot, (carry - c) % out_arr * low, u_next.shape[0], axis=1),
+            u_next,
+            precision=highest,
+        )
     return sums / jnp.maximum(members, 1.0)[:, None, None, None]
 
 

time: 131 us -> 134 us (1.023)
  blocking collectives: 56 us -> 46.7 us
  waiting for transfers between devices: 0.04 us -> 9.19 us
  starting transfers between devices: 0.01 us -> 2.79 us
    all_gather x1 -> x0, blocking collectives: 9.34 us -> none  [body(): everyone = lax.all_gather(profile, 'sta', axis=0, tiled=True)]
    ppermute x0 -> x3, waiting for transfers between devices: none -> 9.15 us  [the longest x2 9.15 us: body(): u_next = lax.ppermute(u_next, 'sta', log)]
    ppermute x0 -> x3, starting transfers between devices: none -> 2.78 us  [the longest x1 2.78 us: body(): block_out = lax.ppermute(block_out, 'sta', found)]
  transfers between devices with their start and end apart: 1 -> 4, of which waited for: 0 -> 2; matrix products, arithmetic and copies ran while one was open for 6% -> 7% of each run, Pallas kernels for 0% -> 0%
where the time goes in v1:
time: 134 us
  blocking collectives  46.7 us (35%)
  local copies, waits for them, and re-layouts  35.7 us (27%)
  other arithmetic  15.8 us (12%)
  between operations  13.6 us (10%)
  matrix products  9.76 us (7%)
  waiting for transfers between devices  9.19 us (7%)
  starting transfers between devices  2.79 us (2%)
    psum x1, blocking collectives, body(): normal = lax.psum(normal_part, 'evt') + jnp.eye(5, dtype=jnp.float32)[None]  30.3 us
    reshape x2, local copies, waits for them, and re-layouts, body(): lax.all_gather(solved, 'evt', axis=2, tiled=True)  17.5 us
    all_gather x1, blocking collectives, body(): lax.all_gather(solved, 'evt', axis=2, tiled=True)  16.4 us
    ppermute x2, waiting for transfers between devices, body(): u_next = lax.ppermute(u_next, 'sta', log)  9.15 us
    gather x3, local copies, waits for them, and re-layouts, to_depths(): second = jnp.take_along_axis(values, picks + 1, axis=3)  8.62 us
    gather x3, local copies, waits for them, and re-layouts, to_depths(): first = jnp.take_along_axis(values, picks, axis=3)  8.62 us
    dot_general x1, matrix products, body(): rhs_part = jnp.einsum('sek,sec->skc', weighted, data, precision=highest)  7.27 us
    add x1, other arithmetic, body(): jnp.cos(incidence)[:, :, None] * radial  6.81 us
  transfers between devices with their start and end apart: 4, of which 2 were waited for; matrix products, arithmetic and copies ran while one was open for 7% of the time, Pallas kernels for 0%

profile of v1, /device:TPU:0, one launch (start us, length us, event | category | flops | bytes accessed | tf_op | source)
XLA Modules:
  0.0 133.5 jit_solution(9072047489347087978)
XLA Ops:
  6.5 0.0 reduce-scatter.2.cloned.1.call-start
  6.5 0.8 fusion.25
  7.3 0.7 compare_convert_fusion
  8.0 6.8 %fusion.7 = (f32[8,64,2048]{2,1,0:T(8,128)}, f32[8,64,2048]{2,1,0:T(8,128)}) fusion(bf16[3,8,64,2048]{3,2,1,0:T(8,128)(2,1)} %param.8, f32[8,64]{1,0:T(8,128)S(1)} %get-tuple-element.20, f32[8,64]{1,0:T(8,128)S(1)} %get-tuple-element.15, f32[8,64]{1,0:T(8,128)S(1)} %get-tuple-element.17, f32[8,64]{1,0:T(8,128)S(1)} %get-tuple-element.21), kind=kLoop, calls=%fused_computation.13 | loop fusion | flops 13631488 | bytes 14688256 | tf_op jit(solution)/shard_map/add | solution.py:39
  14.9 0.0 copy-start
  14.9 0.0 copy-start.1
  14.9 7.3 %fusion = f32[8,5,4096]{2,1,0:T(8,128)} fusion(f32[8,64,2048]{2,1,0:T(8,128)} %get-tuple-element.9, f32[8,64,2048]{2,1,0:T(8,128)} %get-tuple-element.8, f32[8,64,5]{1,2,0:T(8,128)S(1)} %stack.19, f32[8,64]{1,0:T(8,128)S(1)} %compare_convert_fusion), kind=kOutput, calls=%fused_computation.2 | convolution fusion | flops 127928832 | bytes 9056256 | tf_op jit(solution)/shard_map/sek,sec->skc/dot_general | solution.py:50
  22.2 0.0 reduce-scatter.2.cloned.1.call-update
  22.2 0.2 fusion.11
  22.5 30.3 %psum.7 = f32[8,5,5]{1,2,0:T(8,128)S(1)} all-reduce(f32[8,5,5]{1,2,0:T(8,128)S(1)} %fusion.11), channel_id=1, replica_groups=mesh['sta'=4,'evt'=8] {'evt'}, use_global_device_ids=true, to_apply=%region_0.0 | all-reduce | flops 200 | bytes 1600 | tf_op jit(solution)/shard_map/psum | solution.py:51
  52.8 0.1 copy.30
  52.9 0.1 copy.31
  53.1 3.7 %custom-call.11 = f32[8,5,5]{2,1,0:T(8,128)S(1)} custom-call(f32[8,5,5]{2,1,0:T(8,128)S(1)} %fusion.18), custom_call_target="Cholesky" | custom-call | tf_op jit(solution)/shard_map/jit(cholesky)/cholesky | solution.py:13
  56.8 0.1 compare_reduce_fusion
  56.9 0.1 select_bitcast_fusion
  57.0 3.2 %custom-call.12 = f32[8,1,5,5]{2,3,1,0:T(8,128)S(1)} custom-call(f32[8,1,5,5]{3,2,1,0:T(8,128)S(1)} %select_bitcast_fusion), custom_call_target="InvertDiagBlocksLowerTriangular" | custom-call | tf_op jit(solution)/shard_map/jit(_solve_triangular)/vmap()/triangular_solve | solution.py:15
  60.2 0.0 copy-done
  60.2 0.1 bitcast_or_fusion.1
  60.3 0.1 reshape.123
  60.4 0.1 reshape.128
  60.4 0.1 and_bitcast_fusion.1
  60.5 0.0 copy-done.1
  60.5 0.2 convert_reduce_fusion
  60.7 0.0 reduce-scatter.2.cloned.1.call-done
  60.8 1.2 fusion.16
  62.0 0.3 fusion.14
  62.2 16.4 %all_gather.3 = f32[8,5,4096]{2,1,0:T(8,128)S(1)} all-gather(f32[8,5,512]{2,1,0:T(8,128)S(1)} %fusion.14), channel_id=1, replica_groups=mesh['sta'=4,'evt'=8] {'evt'}, dimensions={2}, use_global_device_ids=true | all-gather | bytes 737280 | tf_op jit(solution)/shard_map/all_gather | solution.py:54
  78.6 0.6 reshape.136
  79.2 17.0 %copy.34 = f32[8,5,2,2048]{1,2,3,0:T(2,128)} copy(f32[8,5,2,2048]{3,2,1,0:T(2,128)S(1)} %reshape.136) | data formatting | bytes 1310720 | tf_op jit(solution)/shard_map/reshape | solution.py:54
  96.1 8.3 %gather_fusion = f32[512,5,2]{1,2,0:T(2,128)S(1)} fusion(f32[8,5,2,2048]{1,2,3,0:T(2,128)} %copy.34, s32[512]{0:T(512)S(1)} %reshape.123), kind=kCustom, calls=%fused_computation.clone | custom fusion | bytes 45056 | tf_op jit(solution)/shard_map/jit(take_along_axis)/gather | solution.py:20
  104.5 0.2 copy.47
  104.7 8.3 %gather_fusion.1 = f32[512,5,2]{1,2,0:T(2,128)S(1)} fusion(f32[8,5,2,2048]{1,2,3,0:T(2,128)} %copy.34, s32[512]{0:T(512)S(1)} %reshape.128), kind=kCustom, calls=%fused_computation.1.clone | custom fusion | bytes 45056 | tf_op jit(solution)/shard_map/jit(take_along_axis)/gather | solution.py:21
  113.0 0.2 copy.49
  113.3 2.8 %collective-permute-start = (f32[8,5,2,64]{3,0,2,1:T(8,128)S(1)}, f32[8,5,2,64]{3,0,2,1:T(8,128)S(1)}, u32[]{:S(2)}, u32[]{:S(2)}) collective-permute-start(f32[8,5,2,64]{3,0,2,1:T(8,128)S(1)} %fusion.13), channel_id=1, source_target_pairs={{0,24},{8,0},{16,8},{24,16},{1,25},{9,1},{17,9},{25,17},{2,26},{10... | collective-permute-start | bytes 61448 | tf_op jit(solution)/shard_map/ppermute | solution.py:77
  116.0 0.0 collective-permute-start.1
  116.0 0.2 fusion.32
  116.3 4.7 %collective-permute-done.1 = f32[8,5,2,64]{3,0,2,1:T(8,128)S(1)} collective-permute-done((f32[8,5,2,64]{3,0,2,1:T(8,128)S(1)}, f32[8,5,2,64]{3,0,2,1:T(8,128)S(1)}, u32[]{:S(2)}, u32[]{:S(2)}) %collective-permute-start.1) | collective-permute-done | bytes 20512 | tf_op jit(solution)/shard_map/ppermute | solution.py:75
  120.9 0.0 collective-permute-start.2
  120.9 0.0 collective-permute-done
  121.0 0.2 convolution_add_fusion.2
  121.2 0.2 convolution_add_fusion.1
  121.4 4.5 %collective-permute-done.2 = f32[8,5,2,64]{3,0,2,1:T(8,128)S(1)} collective-permute-done((f32[8,5,2,64]{3,0,2,1:T(8,128)S(1)}, f32[8,5,2,64]{3,0,2,1:T(8,128)S(1)}, u32[]{:S(2)}, u32[]{:S(2)}) %collective-permute-start.2) | collective-permute-done | bytes 20512 | tf_op jit(solution)/shard_map/ppermute | solution.py:75
  125.8 0.2 fusion.9
  126.1 0.6 copy.38
  (12 shorter events, 0.1 us)
Async XLA Ops:
  6.5 54.2 %reduce-scatter.2.cloned.1.call-start = ((), (), s32[]{:S(2)}) async-start(), calls=%async_computation.1 | async-start | bytes 1179648 | tf_op jit(solution)/shard_map/reduce_scatter | solution.py:52
  14.9 45.3 %copy-start = (s32[8,512]{1,0:T(8,128)S(1)}, s32[8,512]{1,0:T(8,128)}, u32[]{:S(2)}) copy-start(s32[8,512]{1,0:T(8,128)} %param.12) | copy-start | bytes 49156
  14.9 45.6 %copy-start.1 = (s32[32]{0:T(128)S(1)}, s32[32]{0:T(128)}, u32[]{:S(2)}) copy-start(s32[32]{0:T(128)} %param.13) | copy-start | bytes 388
  113.3 7.7 %collective-permute-start = (f32[8,5,2,64]{3,0,2,1:T(8,128)S(1)}, f32[8,5,2,64]{3,0,2,1:T(8,128)S(1)}, u32[]{:S(2)}, u32[]{:S(2)}) collective-permute-start(f32[8,5,2,64]{3,0,2,1:T(8,128)S(1)} %fusion.13), channel_id=1, source_target_pairs={{0,24},{8,0},{16,8},{24,16},{1,25},{9,1},{17,9},{25,17},{2,26},{10... | collective-permute-start | bytes 61448 | tf_op jit(solution)/shard_map/ppermute | solution.py:77
  116.0 4.9 %collective-permute-start.1 = (f32[8,5,2,64]{3,0,2,1:T(8,128)S(1)}, f32[8,5,2,64]{3,0,2,1:T(8,128)S(1)}, u32[]{:S(2)}, u32[]{:S(2)}) collective-permute-start(f32[8,5,2,64]{3,0,2,1:T(8,128)S(1)} %fusion.13), channel_id=1, source_target_pairs={{0,8},{8,16},{16,24},{24,0},{1,9},{9,17},{17,25},{25,1},{2,10},{10... | collective-permute-start | bytes 61448 | tf_op jit(solution)/shard_map/ppermute | solution.py:75
  120.9 4.9 %collective-permute-start.2 = (f32[8,5,2,64]{3,0,2,1:T(8,128)S(1)}, f32[8,5,2,64]{3,0,2,1:T(8,128)S(1)}, u32[]{:S(2)}, u32[]{:S(2)}) collective-permute-start(f32[8,5,2,64]{3,0,2,1:T(8,128)S(1)} %collective-permute-done.1), channel_id=1, source_target_pairs={{0,8},{8,16},{16,24},{24,0},{1,9},{9,17},{17,25},{25,1},{2,10},{10... | collective-permute-start | bytes 61448 | tf_op jit(solution)/shard_map/ppermute | solution.py:75
Sparse Core Ops, SparseCore 0:
  22.3 35.4 reduce-scatter.1
